TPU v7x, 256 devices: a whole 4x4x8 slice. The times are simulated.
256 devices in a mesh: rows: 128 (over z, x, y), half: 2 (over core).
Axes of the slice: x: 4, y: 4, z: 8, core: 2. Of those that a mesh axis runs over, the one named last changes fastest.
Arguments:
- source_feats: bfloat16 [131072, 1024], P('rows', 'half'), may hold values from -6 to 6
- rel_weight: bfloat16 [3, 2, 512, 512], P(None, 'half'), may hold values from -0.25 to 0.25
- tiles: bfloat16 [4096, 64, 512], P('rows'), may hold values from -0.25 to 0.25
- src_blk: int32 [4096, 8], P('rows'), may hold values from 0 to 15
- rel_id: int32 [4096, 8], P('rows'), may hold values from 0 to 2
- owner: int32 [4096, 1], P('rows'), may hold values from 0 to 127; in each aligned block of 32 rows (0 to 31, 32 to 63, ...) at most 2 rows name the same one
- local_blk: int32 [4096], P('rows'), may hold values from 0 to 31
- in_degree: int32 [262144], P('rows'), may hold values from 1 to 16
- mix_weight: bfloat16 [1024, 1024], P(None, 'half'), may hold values from -0.1875 to 0.1875
- bias: float32 [1024], P('half'), may hold values from -0.5 to 0.5
Outputs:
- out: bfloat16 [262144, 1024], P('rows', 'half')
Inputs may be any that keep to these rules, and one draw needn't show every extreme that they name: Among the 32 rows held by one device along rows, no owner is named more than 2 times, some owner exactly 2 times, and every owner is named somewhere.
All inputs are finite; a program needn't handle non-finite values.
Results may differ from a plain program's by a relative error of at most 0.0054.
Values may be sent and summed in bfloat16 or wider, within the bound.
A program may use at most 128 MiB of HBM per device.

v0:
```python
import jax
import jax.numpy as jnp
from jax import lax
from jax.sharding import PartitionSpec as P


def local(
    source_feats, rel_weight, tiles, src_blk, rel_id, owner, local_blk, in_degree, mix_weight, bias
):
    n_rows = lax.axis_size("rows")
    src_dev, half_w = source_feats.shape
    tile = tiles.shape[1]
    parts, per_row = src_blk.shape
    n_rel = rel_weight.shape[0]
    n_src_blocks = src_dev // tile
    n_blocks = n_rel * n_src_blocks
    n_local = in_degree.shape[0] // tile
    capacity = max(2, 2 * parts // n_rows)
    msgs = jnp.einsum(
        "sj,rjc->rsc", source_feats, rel_weight[:, 0], preferred_element_type=jnp.float32
    ).astype(jnp.bfloat16)
    flat_blocks = msgs.reshape(n_blocks, tile * half_w)
    picks = rel_id * n_src_blocks + src_blk
    per_turn = 16
    block_ids = jnp.arange(n_blocks, dtype=jnp.int32)

    def partial_group(operands):
        group_tiles, group_picks = operands
        chooser = (group_picks.reshape(per_turn * per_row)[:, None] == block_ids[None, :]).astype(
            jnp.bfloat16
        )
        picked = jnp.dot(chooser, flat_blocks, preferred_element_type=jnp.float32).astype(
            jnp.bfloat16
        )
        picked = picked.reshape(per_turn, per_row * tile, half_w)
        return jnp.einsum(
            "pim,pmc->pic", group_tiles, picked, preferred_element_type=jnp.float32
        ).astype(jnp.bfloat16)

    grouped = (
        tiles.reshape(parts // per_turn, per_turn, tile, per_row * tile),
        picks.reshape(parts // per_turn, per_turn, per_row),
    )
    partials = lax.map(partial_group, grouped).reshape(parts, tile * half_w)
    target_dev = owner[:, 0]
    positions = jnp.arange(parts, dtype=jnp.int32)
    earlier = (target_dev[:, None] == target_dev[None, :]) & (
        positions[None, :] < positions[:, None]
    )
    rank = jnp.sum(earlier.astype(jnp.int32), axis=1)
    slot = target_dev * capacity + rank
    slot_ids = jnp.arange(n_rows * capacity, dtype=jnp.int32)
    placing = slot_ids[:, None] == slot[None, :]
    outgoing = jnp.dot(
        placing.astype(jnp.bfloat16), partials, preferred_element_type=jnp.float32
    ).astype(jnp.bfloat16)
    out_ids = jnp.sum(jnp.where(placing, local_blk[None, :] + 1, 0), axis=1) - 1
    block_index = jnp.arange(n_local, dtype=jnp.int32)
    arrived, arrived_ids = (
        lax.all_to_all(outgoing, "rows", split_axis=0, concat_axis=0, tiled=True),
        lax.all_to_all(out_ids, "rows", split_axis=0, concat_axis=0, tiled=True),
    )
    selector = (arrived_ids[None, :] == block_index[:, None]).astype(jnp.bfloat16)
    summed = jnp.dot(selector, arrived, preferred_element_type=jnp.float32)
    summed = summed.reshape(n_local * tile, half_w)
    agg = (summed / in_degree.astype(jnp.float32)[:, None]).astype(jnp.bfloat16)
    mixed = jnp.dot(
        lax.all_gather(agg, "half", axis=1, tiled=True),
        mix_weight,
        preferred_element_type=jnp.float32,
    )
    return jax.nn.relu(mixed + bias).astype(jnp.bfloat16)


def solution(mesh):
    placed = (
        P("rows", "half"),
        P(None, "half", None, None),
        P("rows", None, None),
        P("rows", None),
        P("rows", None),
        P("rows", None),
        P("rows"),
        P("rows"),
        P(None, "half"),
        P("half"),
    )
    return jax.shard_map(
        local, mesh=mesh, in_specs=placed, out_specs=P("rows", "half"), check_vma=False
    )
```

profile of v0, /device:TPU:1, one launch (start us, length us, event | category | flops | bytes accessed | tf_op | source)
XLA Modules:
  0.0 598.6 jit_solution(10182642154321596765)
XLA Ops:
  6.5 0.0 copy-start
  6.5 1.0 convert_reduce_fusion
  7.5 0.7 multiply_add_fusion.1
  8.2 0.1 select_reduce_fusion
  8.3 0.8 sub.7
  9.0 16.3 %all-to-all-start = ((s32[128,2,1]{1,2,0:T(1,128)}), s32[128,2,1]{1,2,0:T(1,128)S(1)}, u32[]{:S(2)}, u32[]{:S(2)}) async-start(s32[128,2,1]{1,2,0:T(1,128)} %bitcast.1), calls=%async_computation | async-start | bytes 131072 | tf_op jit(solution)/shard_map/all_to_all | solution.py:61
  25.4 0.0 copy-done
  25.4 4.8 convert_bitcast_fusion
  30.2 4.7 copy.23
  34.8 0.0 copy-start.3
  34.8 0.0 copy-start.4
  34.8 5.9 reshape.55
  40.7 0.0 copy-done.3
  40.7 0.0 copy-done.4
  40.7 0.1 copy.21
  40.8 54.5 %while.11 = (s32[]{:T(128)}, bf16[2,16,64,512]{3,2,1,0:T(8,128)(2,1)}, bf16[2,16,64,512]{3,2,1,0:T(8,128)(2,1)}, s32[2,16,8]{2,1,0:T(8,128)S(1)}, bf16[48,32768]{1,0:T(8,128)(2,1)}, /*index=5*/s32[]{:T(128)}) while((s32[]{:T(128)}, bf16[2,16,64,512]{3,2,1,0:T(8,128)(2,1)}, bf16[2,16,64,512]{3,2,1,0:T(8,128)(2,1)}, ...), condition=%wide.region_3.4_spmd.clone, body=%wide.region_2.3_spmd.clone.sunk | while | flops 944248832 | bytes 38800968 | solution.py:44
  40.8 0.1 eq.105
  40.9 7.5 %convolution_convert_fusion.4 = bf16[128,32768]{1,0:T(8,128)(2,1)} fusion(bf16[48,32768]{1,0:T(8,128)(2,1)} %get-tuple-element.109, s32[128]{0:T(128)S(1)} %eq.105), kind=kOutput, calls=%fused_computation.1.clone.1 | convolution fusion | flops 406853632 | bytes 11534848 | tf_op jit(solution)/shard_map/while/body/eval_jaxpr/dot_general | solution.py:32
  48.4 13.5 %reshape.70 = bf16[16,512,512]{2,1,0:T(8,128)(2,1)} reshape(bf16[128,32768]{1,0:T(8,128)(2,1)} %convolution_convert_fusion.4) | data formatting | bytes 16777216 | tf_op jit(solution)/shard_map/while/body/eval_jaxpr/reshape | solution.py:35
  61.9 6.1 %fusion.27 = bf16[2,16,64,512]{3,2,1,0:T(8,128)(2,1)} fusion(bf16[2,16,64,512]{3,2,1,0:T(8,128)(2,1)} %get-tuple-element.100, s32[]{:T(128)} %get-tuple-element.99, bf16[16,512,512]{2,1,0:T(8,128)(2,1)} %reshape.70, bf16[2,16,64,512]{3,2,1,0:T(8,128)(2,1)} %get-tuple-element.107), kind=kOutput, calls=%fused_computation.4.clone.1 | convolution fusion | flops 537395200 | bytes 10486784 | tf_op jit(solution)/shard_map/while/body/eval_jaxpr/pim,pmc->pic/dot_general | solution.py:36
  68.0 0.1 eq.105
  68.1 7.5 %convolution_convert_fusion.4 = bf16[128,32768]{1,0:T(8,128)(2,1)} fusion(bf16[48,32768]{1,0:T(8,128)(2,1)} %get-tuple-element.109, s32[128]{0:T(128)S(1)} %eq.105), kind=kOutput, calls=%fused_computation.1.clone.1 | convolution fusion | flops 406853632 | bytes 11534848 | tf_op jit(solution)/shard_map/while/body/eval_jaxpr/dot_general | solution.py:32
  75.6 13.5 %reshape.70 = bf16[16,512,512]{2,1,0:T(8,128)(2,1)} reshape(bf16[128,32768]{1,0:T(8,128)(2,1)} %convolution_convert_fusion.4) | data formatting | bytes 16777216 | tf_op jit(solution)/shard_map/while/body/eval_jaxpr/reshape | solution.py:35
  89.1 6.2 %fusion.27 = bf16[2,16,64,512]{3,2,1,0:T(8,128)(2,1)} fusion(bf16[2,16,64,512]{3,2,1,0:T(8,128)(2,1)} %get-tuple-element.100, s32[]{:T(128)} %get-tuple-element.99, bf16[16,512,512]{2,1,0:T(8,128)(2,1)} %reshape.70, bf16[2,16,64,512]{3,2,1,0:T(8,128)(2,1)} %get-tuple-element.107), kind=kOutput, calls=%fused_computation.4.clone.1 | convolution fusion | flops 537395200 | bytes 10486784 | tf_op jit(solution)/shard_map/while/body/eval_jaxpr/pim,pmc->pic/dot_general | solution.py:36
  95.3 2.8 copy.25
  98.0 8.2 %convolution_convert_fusion.2 = bf16[256,32768]{1,0:T(8,128)(2,1)} fusion(bf16[32,32768]{1,0:T(8,128)(2,1)S(1)} %bitcast.39, s32[32]{0:T(128)S(1)} %get-tuple-element.60), kind=kOutput, calls=%fused_computation.11 | convolution fusion | flops 545267712 | bytes 18874496 | tf_op jit(solution)/shard_map/dot_general | solution.py:54
  106.2 27.0 %all_to_all.13 = bf16[128,2,32768]{2,1,0:T(2,128)(2,1)} reshape(bf16[256,32768]{1,0:T(8,128)(2,1)} %convolution_convert_fusion.2) | data formatting | bytes 33554432 | tf_op jit(solution)/shard_map/all_to_all | solution.py:60
  133.2 0.0 copy-start.2
  133.2 0.0 all-to-all-done
  133.2 14.0 %all-to-all-start.1 = ((bf16[128,2,32768]{2,1,0:T(2,128)(2,1)}), bf16[128,2,32768]{2,1,0:T(2,128)(2,1)}, u32[]{:S(2)}, u32[]{:S(2)}) async-start(bf16[128,2,32768]{2,1,0:T(2,128)(2,1)} %all_to_all.13), calls=%async_computation.1 | async-start | bytes 33554432 | tf_op jit(solution)/shard_map/all_to_all | solution.py:60
  147.2 0.0 all-gather.2.cloned.1.call-start
  147.2 0.0 copy-done.2
  147.3 0.5 broadcast.26
  147.8 0.8 reduce.3
  148.6 0.1 eq.62
  148.7 376.1 %all-to-all-done.1 = bf16[128,2,32768]{2,1,0:T(2,128)(2,1)} async-done(((bf16[128,2,32768]{2,1,0:T(2,128)(2,1)}), bf16[128,2,32768]{2,1,0:T(2,128)(2,1)}, u32[]{:S(2)}, u32[]{:S(2)}) %all-to-all-start.1) | async-done | bytes 16777248 | tf_op jit(solution)/shard_map/all_to_all | solution.py:60
  524.8 25.0 %all_to_all.15 = bf16[256,32768]{1,0:T(8,128)(2,1)} reshape(bf16[128,2,32768]{2,1,0:T(2,128)(2,1)} %all-to-all-done.1) | data formatting | bytes 33554432 | tf_op jit(solution)/shard_map/all_to_all | solution.py:60
  549.8 10.6 %fusion.10 = f32[32,32768]{1,0:T(8,128)} fusion(bf16[256,32768]{1,0:T(8,128)(2,1)} %all_to_all.15, s32[256]{0:T(256)S(1)} %eq.62), kind=kOutput, calls=%fused_computation.20 | convolution fusion | flops 536879104 | bytes 20972544 | tf_op jit(solution)/shard_map/dot_general | solution.py:64
  560.4 4.9 reshape.57
  565.3 0.0 copy-start.5
  565.3 0.0 copy-start.6
  565.3 4.0 divide_convert_fusion
  569.3 0.0 all-gather.2.cloned.1.call-update
  569.3 16.5 %all-gather.2.cloned.1.call-done = bf16[2048,1024]{1,0:T(8,128)(2,1)} async-done(((bf16[2048,512]{1,0:T(8,128)(2,1)}), bf16[2048,1024]{1,0:T(8,128)(2,1)}) %all-gather.2.cloned.1.call-update) | async-done | bytes 4194320 | tf_op jit(solution)/shard_map/all_gather | solution.py:68
  585.8 0.0 copy-done.5
  585.8 0.0 copy-done.6
  585.8 0.0 copy-start.1
  585.8 6.0 maximum_convert_fusion
  591.8 0.0 copy-done.1
  (6 shorter events, 0.0 us)
Async XLA Ops:
  6.5 18.9 %copy-start = (bf16[3,1,512,512]{3,2,1,0:T(8,128)(2,1)S(1)}, bf16[3,1,512,512]{3,2,1,0:T(8,128)(2,1)}, u32[]{:S(2)}) copy-start(bf16[3,1,512,512]{3,2,1,0:T(8,128)(2,1)} %param.13) | copy-start | bytes 4718596
  9.0 124.1 %all-to-all-start = ((s32[128,2,1]{1,2,0:T(1,128)}), s32[128,2,1]{1,2,0:T(1,128)S(1)}, u32[]{:S(2)}, u32[]{:S(2)}) async-start(s32[128,2,1]{1,2,0:T(1,128)} %bitcast.1), calls=%async_computation | async-start | bytes 131072 | tf_op jit(solution)/shard_map/all_to_all | solution.py:61
  34.8 5.9 copy-start.3
  34.8 5.9 copy-start.4
  133.2 14.1 %copy-start.2 = (s32[2048]{0:T(1024)S(1)}, s32[2048]{0:T(1024)}, u32[]{:S(2)}) copy-start(s32[2048]{0:T(1024)} %param.19) | copy-start | bytes 24580
  133.2 391.7 %all-to-all-start.1 = ((bf16[128,2,32768]{2,1,0:T(2,128)(2,1)}), bf16[128,2,32768]{2,1,0:T(2,128)(2,1)}, u32[]{:S(2)}, u32[]{:S(2)}) async-start(bf16[128,2,32768]{2,1,0:T(2,128)(2,1)} %all_to_all.13), calls=%async_computation.1 | async-start | bytes 33554432 | tf_op jit(solution)/shard_map/all_to_all | solution.py:60
  147.2 438.6 %all-gather.2.cloned.1.call-start = ((), (), s32[]{:S(2)}) async-start(), calls=%async_computation.2 | async-start | bytes 6291456 | tf_op jit(solution)/shard_map/all_gather | solution.py:68
  565.3 20.5 %copy-start.5 = (bf16[1024,512]{1,0:T(8,128)(2,1)S(1)}, bf16[1024,512]{1,0:T(8,128)(2,1)}, u32[]{:S(2)}) copy-start(bf16[1024,512]{1,0:T(8,128)(2,1)} %param.20) | copy-start | bytes 3145732
  565.3 20.5 %copy-start.6 = (f32[512]{0:T(512)S(1)}, f32[512]{0:T(512)}, u32[]{:S(2)}) copy-start(f32[512]{0:T(512)} %param.21) | copy-start | bytes 6148
  585.8 6.0 copy-start.1
Sparse Core Ops, SparseCore 0:
  569.4 16.2 all-gather.1
where the time goes:
time: 601 us; the launch traced here: 599 us
  waiting for transfers between devices  393 us (65%)
  local copies, waits for them, and re-layouts  98.9 us (16%)
  matrix products  56.8 us (9%)
  starting transfers between devices  30.4 us (5%)
  between operations  13.5 us (2%)
  other arithmetic  6.52 us (1%)
    all_to_all x1, waiting for transfers between devices, local(): lax.all_to_all(outgoing, 'rows', split_axis=0, concat_axis=0, tiled=True)  376 us
    all_to_all x2, local copies, waits for them, and re-layouts, local(): lax.all_to_all(outgoing, 'rows', split_axis=0, concat_axis=0, tiled=True)  52 us
    reshape x2, local copies, waits for them, and re-layouts, partial_group(): picked = picked.reshape(per_turn, per_row * tile, half_w)  26.9 us
    all_gather x1, waiting for transfers between devices, local(): lax.all_gather(agg, 'half', axis=1, tiled=True)  16.5 us
    all_to_all x1, starting transfers between devices, local(): lax.all_to_all(out_ids, 'rows', split_axis=0, concat_axis=0, tiled=True)  16.3 us
    dot_general x2, matrix products, partial_group(): jnp.dot(chooser, flat_blocks, preferred_element_type=jnp.float32)  15 us
    all_to_all x1, starting transfers between devices, local(): lax.all_to_all(outgoing, 'rows', split_axis=0, concat_axis=0, tiled=True)  14 us
    dot_general x2, matrix products, partial_group(): jnp.einsum('pim,pmc->pic', group_tiles, picked, preferred_element_type=jn...  12.3 us
  transfers between devices with their start and end apart: 3, of which 2 were waited for; matrix products, arithmetic and copies ran while one was open for 14% of the time, Pallas kernels for 0%

commit v1 on v0

--- a/solution.py
+++ b/solution.py
@@ -64,11 +64,16 @@
     summed = jnp.dot(selector, arrived, preferred_element_type=jnp.float32)
     summed = summed.reshape(n_local * tile, half_w)
     agg = (summed / in_degree.astype(jnp.float32)[:, None]).astype(jnp.bfloat16)
-    mixed = jnp.dot(
-        lax.all_gather(agg, "half", axis=1, tiled=True),
-        mix_weight,
-        preferred_element_type=jnp.float32,
-    )
+
+    def edit_roads_here(z_in, axis_key):
+        return jnp.concatenate(
+            lax.all_to_all(
+                jnp.stack(tuple((z_in for _ in range(lax.psum(1, axis_key))))), axis_key, 0, 0
+            ),
+            1,
+        )
+
+    mixed = jnp.dot(edit_roads_here(agg, "half"), mix_weight, preferred_element_type=jnp.float32)
     return jax.nn.relu(mixed + bias).astype(jnp.bfloat16)
 
 

time: 601 us -> 582 us (0.968)
  waiting for transfers between devices: 393 us -> 376 us
  between operations: 13.5 us -> 0.11 us
  blocking collectives: 0 us -> 8.08 us
    all_gather x1 -> x0, waiting for transfers between devices: 16.5 us -> none  [local(): lax.all_gather(agg, 'half', axis=1, tiled=True)]
    all_to_all x0 -> x1, blocking collectives: none -> 8.08 us  [edit_roads_here(): lax.all_to_all(jnp.stack(tuple((z_in for _ in range(lax.psum(1, axis_key)...]
  transfers between devices with their start and end apart: 3 -> 2, of which waited for: 2 -> 1; matrix products, arithmetic and copies ran while one was open for 14% -> 14% of each run, Pallas kernels for 0% -> 0%
where the time goes in v1:
time: 582 us; the launch traced here: 579 us
  waiting for transfers between devices  376 us (65%)
  local copies, waits for them, and re-layouts  104 us (18%)
  matrix products  54.5 us (9%)
  starting transfers between devices  30.4 us (5%)
  blocking collectives  8.08 us (1%)
    all_to_all x1, waiting for transfers between devices, local(): lax.all_to_all(outgoing, 'rows', split_axis=0, concat_axis=0, tiled=True)  376 us
    all_to_all x2, local copies, waits for them, and re-layouts, local(): lax.all_to_all(outgoing, 'rows', split_axis=0, concat_axis=0, tiled=True)  52 us
    reshape x2, local copies, waits for them, and re-layouts, partial_group(): picked = picked.reshape(per_turn, per_row * tile, half_w)  26.9 us
    all_to_all x1, starting transfers between devices, local(): lax.all_to_all(out_ids, 'rows', split_axis=0, concat_axis=0, tiled=True)  16.3 us
    dot_general x2, matrix products, partial_group(): jnp.dot(chooser, flat_blocks, preferred_element_type=jnp.float32)  15 us
    all_to_all x1, starting transfers between devices, local(): lax.all_to_all(outgoing, 'rows', split_axis=0, concat_axis=0, tiled=True)  14 us
    dot_general x2, matrix products, partial_group(): jnp.einsum('pim,pmc->pic', group_tiles, picked, preferred_element_type=jn...  12.3 us
  transfers between devices with their start and end apart: 2, of which 1 were waited for; matrix products, arithmetic and copies ran while one was open for 14% of the time, Pallas kernels for 0%

profile of v1, /device:TPU:1, one launch (start us, length us, event | category | flops | bytes accessed | tf_op | source)
XLA Modules:
  0.0 579.2 jit_solution(13426691568418394700)
XLA Ops:
  0.0 0.0 copy-start
  0.0 1.0 convert_reduce_fusion
  1.0 0.7 multiply_add_fusion.1
  1.7 0.1 select_reduce_fusion
  1.8 0.8 sub.7
  2.5 16.3 %all-to-all-start = ((s32[128,2,1]{1,2,0:T(1,128)}), s32[128,2,1]{1,2,0:T(1,128)S(1)}, u32[]{:S(2)}, u32[]{:S(2)}) async-start(s32[128,2,1]{1,2,0:T(1,128)} %bitcast.1), calls=%async_computation | async-start | bytes 131072 | tf_op jit(solution)/shard_map/all_to_all | solution.py:61
  18.9 0.0 copy-done
  18.9 4.8 convert_bitcast_fusion
  23.6 4.7 copy.25
  28.3 0.0 copy-start.3
  28.3 0.0 copy-start.4
  28.3 5.9 %reshape.91 = bf16[48,32768]{1,0:T(8,128)(2,1)} reshape(bf16[3,1024,512]{2,1,0:T(8,128)(2,1)} %copy.25) | data formatting | bytes 6291456 | tf_op jit(solution)/shard_map/reshape | solution.py:22
  34.3 0.0 copy-done.3
  34.3 0.0 copy-done.4
  34.3 0.1 copy.23
  34.3 54.4 %while.11 = (s32[]{:T(128)}, bf16[2,16,64,512]{3,2,1,0:T(8,128)(2,1)}, bf16[2,16,64,512]{3,2,1,0:T(8,128)(2,1)}, s32[2,16,8]{2,1,0:T(8,128)S(1)}, bf16[48,32768]{1,0:T(8,128)(2,1)}, /*index=5*/s32[]{:T(128)}) while((s32[]{:T(128)}, bf16[2,16,64,512]{3,2,1,0:T(8,128)(2,1)}, bf16[2,16,64,512]{3,2,1,0:T(8,128)(2,1)}, ...), condition=%wide.region_3.4_spmd.clone, body=%wide.region_2.3_spmd.clone.sunk | while | flops 944248832 | bytes 38800968 | solution.py:44
  34.4 0.1 eq.105
  34.4 7.5 %convolution_convert_fusion.4 = bf16[128,32768]{1,0:T(8,128)(2,1)} fusion(bf16[48,32768]{1,0:T(8,128)(2,1)} %get-tuple-element.109, s32[128]{0:T(128)S(1)} %eq.105), kind=kOutput, calls=%fused_computation.1.clone.1 | convolution fusion | flops 406853632 | bytes 11534848 | tf_op jit(solution)/shard_map/while/body/eval_jaxpr/dot_general | solution.py:32
  41.9 13.5 %reshape.108 = bf16[16,512,512]{2,1,0:T(8,128)(2,1)} reshape(bf16[128,32768]{1,0:T(8,128)(2,1)} %convolution_convert_fusion.4) | data formatting | bytes 16777216 | tf_op jit(solution)/shard_map/while/body/eval_jaxpr/reshape | solution.py:35
  55.4 6.1 %fusion.27 = bf16[2,16,64,512]{3,2,1,0:T(8,128)(2,1)} fusion(bf16[2,16,64,512]{3,2,1,0:T(8,128)(2,1)} %get-tuple-element.100, s32[]{:T(128)} %get-tuple-element.99, bf16[16,512,512]{2,1,0:T(8,128)(2,1)} %reshape.108, bf16[2,16,64,512]{3,2,1,0:T(8,128)(2,1)} %get-tuple-element.107), kind=kOutput, calls=%fused_computation.4.clone.1 | convolution fusion | flops 537395200 | bytes 10486784 | tf_op jit(solution)/shard_map/while/body/eval_jaxpr/pim,pmc->pic/dot_general | solution.py:36
  61.5 0.1 eq.105
  61.6 7.5 %convolution_convert_fusion.4 = bf16[128,32768]{1,0:T(8,128)(2,1)} fusion(bf16[48,32768]{1,0:T(8,128)(2,1)} %get-tuple-element.109, s32[128]{0:T(128)S(1)} %eq.105), kind=kOutput, calls=%fused_computation.1.clone.1 | convolution fusion | flops 406853632 | bytes 11534848 | tf_op jit(solution)/shard_map/while/body/eval_jaxpr/dot_general | solution.py:32
  69.1 13.5 %reshape.108 = bf16[16,512,512]{2,1,0:T(8,128)(2,1)} reshape(bf16[128,32768]{1,0:T(8,128)(2,1)} %convolution_convert_fusion.4) | data formatting | bytes 16777216 | tf_op jit(solution)/shard_map/while/body/eval_jaxpr/reshape | solution.py:35
  82.6 6.1 %fusion.27 = bf16[2,16,64,512]{3,2,1,0:T(8,128)(2,1)} fusion(bf16[2,16,64,512]{3,2,1,0:T(8,128)(2,1)} %get-tuple-element.100, s32[]{:T(128)} %get-tuple-element.99, bf16[16,512,512]{2,1,0:T(8,128)(2,1)} %reshape.108, bf16[2,16,64,512]{3,2,1,0:T(8,128)(2,1)} %get-tuple-element.107), kind=kOutput, calls=%fused_computation.4.clone.1 | convolution fusion | flops 537395200 | bytes 10486784 | tf_op jit(solution)/shard_map/while/body/eval_jaxpr/pim,pmc->pic/dot_general | solution.py:36
  88.7 2.8 copy.28
  91.5 8.2 %convolution_convert_fusion.2 = bf16[256,32768]{1,0:T(8,128)(2,1)} fusion(bf16[32,32768]{1,0:T(8,128)(2,1)S(1)} %bitcast.42, s32[32]{0:T(128)S(1)} %get-tuple-element.60), kind=kOutput, calls=%fused_computation.11 | convolution fusion | flops 545267712 | bytes 18874496 | tf_op jit(solution)/shard_map/dot_general | solution.py:54
  99.7 27.0 %all_to_all.16 = bf16[128,2,32768]{2,1,0:T(2,128)(2,1)} reshape(bf16[256,32768]{1,0:T(8,128)(2,1)} %convolution_convert_fusion.2) | data formatting | bytes 33554432 | tf_op jit(solution)/shard_map/all_to_all | solution.py:60
  126.7 0.0 copy-start.2
  126.7 0.0 all-to-all-done
  126.7 14.0 %all-to-all-start.1 = ((bf16[128,2,32768]{2,1,0:T(2,128)(2,1)}), bf16[128,2,32768]{2,1,0:T(2,128)(2,1)}, u32[]{:S(2)}, u32[]{:S(2)}) async-start(bf16[128,2,32768]{2,1,0:T(2,128)(2,1)} %all_to_all.16), calls=%async_computation.1 | async-start | bytes 33554432 | tf_op jit(solution)/shard_map/all_to_all | solution.py:60
  140.7 0.0 copy-done.2
  140.7 0.5 broadcast.40
  141.2 0.8 reduce.3
  142.1 0.1 eq.62
  142.2 376.1 %all-to-all-done.1 = bf16[128,2,32768]{2,1,0:T(2,128)(2,1)} async-done(((bf16[128,2,32768]{2,1,0:T(2,128)(2,1)}), bf16[128,2,32768]{2,1,0:T(2,128)(2,1)}, u32[]{:S(2)}, u32[]{:S(2)}) %all-to-all-start.1) | async-done | bytes 16777248 | tf_op jit(solution)/shard_map/all_to_all | solution.py:60
  518.3 25.0 %all_to_all.18 = bf16[256,32768]{1,0:T(8,128)(2,1)} reshape(bf16[128,2,32768]{2,1,0:T(2,128)(2,1)} %all-to-all-done.1) | data formatting | bytes 33554432 | tf_op jit(solution)/shard_map/all_to_all | solution.py:60
  543.3 10.6 %fusion.10 = f32[32,32768]{1,0:T(8,128)} fusion(bf16[256,32768]{1,0:T(8,128)(2,1)} %all_to_all.18, s32[256]{0:T(256)S(1)} %eq.62), kind=kOutput, calls=%fused_computation.21 | convolution fusion | flops 536879104 | bytes 20972544 | tf_op jit(solution)/shard_map/dot_general | solution.py:64
  553.9 4.9 reshape.93
  558.8 5.5 copy.26
  564.3 2.7 divide_convert_fusion
  567.0 0.4 pad_maximum_fusion
  567.4 0.0 copy-start.5
  567.4 0.0 copy-start.6
  567.4 8.1 %all_to_all.23 = bf16[2,2048,512]{1,2,0:T(8,128)(2,1)S(1)} all-to-all(bf16[2,2048,512]{1,2,0:T(8,128)(2,1)S(1)} %pad_maximum_fusion), channel_id=1, replica_groups=mesh['rows'=128,'half'=2] {'half'}, dimensions={0} | all-to-all | bytes 8388608 | tf_op jit(solution)/shard_map/all_to_all | solution.py:70
  575.5 0.0 copy-start.1
  575.5 0.0 copy-done.5
  575.5 0.0 copy-done.6
  575.5 3.8 maximum_convert_fusion
  579.2 0.0 copy-done.1
  (6 shorter events, 0.0 us)
Async XLA Ops:
  0.0 18.9 %copy-start = (bf16[3,1,512,512]{3,2,1,0:T(8,128)(2,1)S(1)}, bf16[3,1,512,512]{3,2,1,0:T(8,128)(2,1)}, u32[]{:S(2)}) copy-start(bf16[3,1,512,512]{3,2,1,0:T(8,128)(2,1)} %param.13) | copy-start | bytes 4718596
  2.5 124.1 %all-to-all-start = ((s32[128,2,1]{1,2,0:T(1,128)}), s32[128,2,1]{1,2,0:T(1,128)S(1)}, u32[]{:S(2)}, u32[]{:S(2)}) async-start(s32[128,2,1]{1,2,0:T(1,128)} %bitcast.1), calls=%async_computation | async-start | bytes 131072 | tf_op jit(solution)/shard_map/all_to_all | solution.py:61
  28.3 5.9 %copy-start.3 = (s32[32,8]{0,1:T(8,128)S(1)}, s32[32,8]{0,1:T(8,128)}, u32[]{:S(2)}) copy-start(s32[32,8]{0,1:T(8,128)} %param.15) | copy-start | bytes 3076
  28.3 5.9 %copy-start.4 = (s32[32,8]{0,1:T(8,128)S(1)}, s32[32,8]{0,1:T(8,128)}, u32[]{:S(2)}) copy-start(s32[32,8]{0,1:T(8,128)} %param.16) | copy-start | bytes 3076
  126.7 14.1 %copy-start.2 = (s32[2048]{0:T(1024)S(1)}, s32[2048]{0:T(1024)}, u32[]{:S(2)}) copy-start(s32[2048]{0:T(1024)} %param.19) | copy-start | bytes 24580
  126.7 391.6 %all-to-all-start.1 = ((bf16[128,2,32768]{2,1,0:T(2,128)(2,1)}), bf16[128,2,32768]{2,1,0:T(2,128)(2,1)}, u32[]{:S(2)}, u32[]{:S(2)}) async-start(bf16[128,2,32768]{2,1,0:T(2,128)(2,1)} %all_to_all.16), calls=%async_computation.1 | async-start | bytes 33554432 | tf_op jit(solution)/shard_map/all_to_all | solution.py:60
  567.4 8.1 %copy-start.5 = (bf16[1024,512]{1,0:T(8,128)(2,1)S(1)}, bf16[1024,512]{1,0:T(8,128)(2,1)}, u32[]{:S(2)}) copy-start(bf16[1024,512]{1,0:T(8,128)(2,1)} %param.20) | copy-start | bytes 3145732
  567.4 8.1 %copy-start.6 = (f32[512]{0:T(512)S(1)}, f32[512]{0:T(512)}, u32[]{:S(2)}) copy-start(f32[512]{0:T(512)} %param.21) | copy-start | bytes 6148
  575.5 3.8 copy-start.1
